TPU v7x, 32 devices: a whole 2x2x4 slice. The times are simulated.
32 devices in a mesh: row: 8 (over y, x, core), col: 4 (over z).
Axes of the slice: x: 2, y: 2, z: 4, core: 2. Of those that a mesh axis runs over, the one named last changes fastest.
Arguments:
- x_mat: float32 [512, 512], replicated, may hold values from -8 to 40, as said below
- y_inv: float32 [512, 512], replicated, may hold values from -8 to 40, as said below
- panel_blocks: bfloat16 [512, 4096], replicated, may hold values from -6 to 6
- panel_pos: int32 [512], replicated, may hold values from 0 to 63
- group_blocks: int32 [32, 2], replicated, may hold values from 0 to 63
- cons_blocks: bfloat16 [57344, 4096], P(('row', 'col')), may hold values from -6 to 6
- slot_block: int32 [57344], P(('row', 'col')), may hold values from 0 to 1
- slot_row: int32 [57344], P(('row', 'col')), may hold values from 0 to 32767, as said below
- group_size: int32 [32], P(('row', 'col')), may hold values from 768 to 1792, as said below
- trailing: float32 [32768, 2048], P('row', 'col'), may hold values from -6 to 6
Outputs:
- lower_panel: float32 [32768, 512], P(('row', 'col'))
- updated: float32 [32768, 2048], P('row', 'col')
Inputs may be any that keep to these rules, and one draw needn't show every extreme that they name: `x_mat`: symmetric positive definite. `y_inv`: symmetric positive definite. `slot_row`: over all groups, the live slots hold every row 0 to 32767 exactly once; the live slots of one group hold at most 56 rows of one aligned range of 1024 rows, and that most is reached in every draw; other slots hold arbitrary rows. `group_size`: the live slots of a group are its first slots; some group has exactly 1792 in every draw.
All inputs are finite; a program needn't handle non-finite values.
Results may differ from a plain program's by a relative error of at most 0.004.
Values may be sent and summed in bfloat16 or wider, within the bound.
A program may use at most 192 MiB of HBM per device.

v0:
```python
import math
import jax
import jax.numpy as jnp
from jax import lax
from jax.sharding import PartitionSpec as P


def build_h(values, position, x_mat, y_inv):
    highest = lax.Precision.HIGHEST
    matrix_order = x_mat.shape[0]
    block_size = math.isqrt(values.shape[0])
    block_count = matrix_order // block_size
    e_mat = values.reshape(block_size, block_size).astype(jnp.float32)
    row_start = position // block_count * block_size
    col_start = position % block_count * block_size
    x_left = lax.dynamic_slice_in_dim(x_mat, row_start, block_size, 1)
    x_right = lax.dynamic_slice_in_dim(x_mat, col_start, block_size, 1)
    y_low = lax.dynamic_slice_in_dim(y_inv, col_start, block_size, 0)
    y_high = lax.dynamic_slice_in_dim(y_inv, row_start, block_size, 0)
    term_one = jnp.dot(jnp.dot(x_left, e_mat, precision=highest), y_low, precision=highest)
    term_two = jnp.dot(jnp.dot(x_right, e_mat.T, precision=highest), y_high, precision=highest)
    g_mat = term_one + term_two
    h_mat = (g_mat + g_mat.T).astype(jnp.bfloat16)
    h_mat = h_mat.reshape(block_count, block_size, block_count, block_size).transpose(0, 2, 1, 3)
    return h_mat.reshape(block_count * block_count, block_size * block_size)


def body(
    x_mat,
    y_inv,
    panel_blocks,
    panel_pos,
    group_blocks,
    cons_blocks,
    slot_block,
    slot_row,
    group_size,
    trailing,
):
    rows_size = lax.axis_size("row")
    cols_size = lax.axis_size("col")
    devices = rows_size * cols_size
    col_index = lax.axis_index("col")
    device_id = lax.axis_index("row") * cols_size + col_index
    panel_cols = panel_blocks.shape[0]
    per_device = panel_cols // devices
    own_values = lax.dynamic_slice_in_dim(panel_blocks, device_id * per_device, per_device, 0)
    own_pos = lax.dynamic_slice_in_dim(panel_pos, device_id * per_device, per_device, 0)
    own_blocks = jax.vmap(build_h, in_axes=(0, 0, None, None))(own_values, own_pos, x_mat, y_inv)
    chosen = jnp.take(own_blocks, panel_pos, axis=1)
    column_part = jnp.einsum("if,nif->in", panel_blocks, chosen, preferred_element_type=jnp.float32)
    panel_schur = lax.all_gather(column_part, ("row", "col"), axis=1, tiled=True)
    symmetric = 0.5 * (panel_schur + panel_schur.T)
    diag_shift = 0.01 * jnp.mean(jnp.diagonal(symmetric))
    factor = jnp.linalg.cholesky(symmetric + diag_shift * jnp.eye(panel_cols, dtype=jnp.float32))
    slot_count = cons_blocks.shape[0]
    outgoing = jnp.take(own_blocks, group_blocks.T, axis=1)
    received = lax.all_to_all(outgoing, ("row", "col"), split_axis=2, concat_axis=2, tiled=True)
    running = jnp.zeros((slot_count, received.shape[2], received.shape[0]), jnp.float32)
    for slot_index in range(received.shape[1]):
        product_part = jnp.einsum(
            "sf,ndf->sdn", cons_blocks, received[:, slot_index], preferred_element_type=jnp.float32
        )
        running = jnp.where((slot_block == slot_index)[:, None, None], product_part, running)
    schur_rows = running.reshape(slot_count, panel_cols)
    sub_rows = trailing.shape[0] // cols_size
    base_share = sub_rows // devices
    spread = sub_rows - devices // 4 * base_share
    capacity = base_share + (spread + devices - 1) // devices
    live_slots = jnp.arange(slot_count, dtype=jnp.int32) < group_size[0]
    target = slot_row // sub_rows
    dest_hits = (
        (target[:, None] == jnp.arange(devices, dtype=jnp.int32)[None, :]) & live_slots[:, None]
    ).astype(jnp.int32)
    before = jnp.cumsum(dest_hits, axis=0) - dest_hits
    dest_rank = jnp.sum(before * dest_hits, axis=1)
    slot_place = jnp.where(live_slots, target * capacity + dest_rank, devices * capacity)
    send_rows = (
        jnp.zeros((devices * capacity, panel_cols), jnp.float32)
        .at[slot_place]
        .set(schur_rows, mode="drop")
    )
    send_local = (
        jnp.full((devices * capacity,), sub_rows, jnp.int32)
        .at[slot_place]
        .set(slot_row % sub_rows, mode="drop")
    )
    recv_rows, recv_local = (
        lax.all_to_all(
            send_rows.reshape(devices, capacity, panel_cols),
            ("row", "col"),
            split_axis=0,
            concat_axis=0,
            tiled=True,
        ),
        lax.all_to_all(
            send_local.reshape(devices, capacity),
            ("row", "col"),
            split_axis=0,
            concat_axis=0,
            tiled=True,
        ),
    )
    row_slab = (
        jnp.zeros((sub_rows, panel_cols), jnp.float32)
        .at[recv_local.reshape(-1)]
        .set(recv_rows.reshape(-1, panel_cols), mode="drop")
    )
    lower_slab = lax.linalg.triangular_solve(
        factor, row_slab, left_side=False, lower=True, transpose_a=True
    )
    all_rows = lax.all_gather(lower_slab, "col", axis=0, tiled=True)
    block_rows = trailing.shape[1] // rows_size
    own_rows = lax.dynamic_slice_in_dim(all_rows, col_index * block_rows, block_rows, 0)
    picked = lax.all_gather(own_rows, "row", axis=0, tiled=True)
    updated = trailing - jnp.dot(all_rows, picked.T, precision=lax.Precision.HIGHEST)
    return (lower_slab, updated)


def solution(mesh):
    return jax.shard_map(
        body,
        mesh=mesh,
        in_specs=(
            P(),
            P(),
            P(),
            P(),
            P(),
            P(("row", "col"), None),
            P(("row", "col")),
            P(("row", "col")),
            P(("row", "col")),
            P("row", "col"),
        ),
        out_specs=(P(("row", "col"), None), P("row", "col")),
        check_vma=False,
    )
```

profile of v0, /device:TPU:0, one launch (start us, length us, event | category | flops | bytes accessed | tf_op | source)
XLA Modules:
  0.0 992.5 jit_solution(9979744026841548414)
XLA Ops:
  10.2 2.5 broadcast.301.clone
  12.6 31.8 %while.5 = (s32[]{:T(128)}, f32[512,512]{1,0:T(8,128)S(1)}, s32[16,2]{0,1:T(2,128)S(1)}, f32[16,512,64]{2,1,0:T(8,128)}, s32[]{:T(128)}) while((s32[]{:T(128)}, f32[512,512]{1,0:T(8,128)S(1)}, s32[16,2]{0,1:T(2,128)S(1)}, f32[16,512,64]{2,1,0:T(8,128)}, s32[]{:T(128)}) %tuple.108), condition=%wide.while_cond, body=%wide.while_body.sunk | while | flops 2 | bytes 394329 | solution.py:16
  45.8 34.9 %while.6 = (s32[]{:T(128)}, f32[512,512]{1,0:T(8,128)}, s32[16,2]{0,1:T(2,128)S(1)}, f32[16,64,512]{2,1,0:T(8,128)S(1)}, s32[]{:T(128)}) while((s32[]{:T(128)}, f32[512,512]{1,0:T(8,128)}, s32[16,2]{0,1:T(2,128)S(1)}, f32[16,64,512]{2,1,0:T(8,128)S(1)}, s32[]{:T(128)}) %tuple.90), condition=%wide.while_cond.1, body=%wide.while_body.1.sunk | while | flops 2 | bytes 262241 | solution.py:18
  80.8 2.6 broadcast.301.clone.1
  83.4 35.3 %while.7 = (s32[]{:T(128)}, f32[512,512]{1,0:T(8,128)S(1)}, s32[16,2]{0,1:T(2,128)S(1)}, f32[16,512,64]{2,1,0:T(8,128)}, s32[]{:T(128)}) while((s32[]{:T(128)}, f32[512,512]{1,0:T(8,128)S(1)}, s32[16,2]{0,1:T(2,128)S(1)}, f32[16,512,64]{2,1,0:T(8,128)}, s32[]{:T(128)}) %tuple.109), condition=%wide.while_cond.2, body=%wide.while_body.2.sunk | while | flops 2 | bytes 394329 | solution.py:17
  118.7 5.0 fusion.71
  123.8 4.1 fusion.73
  129.4 47.0 %while.8 = (s32[]{:T(128)}, f32[512,512]{1,0:T(8,128)}, s32[16,2]{0,1:T(2,128)S(1)}, f32[16,64,512]{2,1,0:T(8,128)}, s32[]{:T(128)}) while((s32[]{:T(128)}, f32[512,512]{1,0:T(8,128)}, s32[16,2]{0,1:T(2,128)S(1)}, f32[16,64,512]{2,1,0:T(8,128)}, s32[]{:T(128)}) %tuple.110), condition=%wide.while_cond.3, body=%wide.while_body.3.sunk | while | flops 2 | bytes 263257 | solution.py:19
  130.1 2.3 bitcast_dynamic-update-slice_fusion.13
  133.0 2.3 bitcast_dynamic-update-slice_fusion.13
  136.0 2.3 bitcast_dynamic-update-slice_fusion.13
  138.9 2.3 bitcast_dynamic-update-slice_fusion.13
  141.9 2.3 bitcast_dynamic-update-slice_fusion.13
  144.8 2.3 bitcast_dynamic-update-slice_fusion.13
  147.7 2.3 bitcast_dynamic-update-slice_fusion.13
  150.6 2.3 bitcast_dynamic-update-slice_fusion.13
  153.6 2.3 bitcast_dynamic-update-slice_fusion.13
  156.5 2.3 bitcast_dynamic-update-slice_fusion.13
  159.5 2.3 bitcast_dynamic-update-slice_fusion.13
  162.4 2.3 bitcast_dynamic-update-slice_fusion.13
  165.3 2.3 bitcast_dynamic-update-slice_fusion.13
  168.3 2.3 bitcast_dynamic-update-slice_fusion.13
  171.2 2.3 bitcast_dynamic-update-slice_fusion.13
  174.1 2.3 bitcast_dynamic-update-slice_fusion.13
  176.4 17.1 %fusion.72 = f32[16,512,512]{2,1,0:T(8,128)} fusion(f32[16,512,64]{1,2,0:T(8,128)S(1)} %fusion.71, f32[16,64,512]{2,1,0:T(8,128)} %copy-done.3), kind=kOutput, calls=%fused_computation.160 | convolution fusion | flops 3221225472 | bytes 20971520 | tf_op jit(solution)/shard_map/vmap()/dot_general | solution.py:20
  193.5 18.9 %convolution_add_fusion = f32[16,512,512]{2,1,0:T(8,128)} fusion(f32[16,512,512]{2,1,0:T(8,128)} %fusion.72, f32[16,512,64]{1,2,0:T(8,128)S(1)} %copy-done.2, f32[16,64,512]{2,1,0:T(8,128)S(1)} %copy-done.4), kind=kOutput, calls=%fused_computation.28 | convolution fusion | flops 3225419776 | bytes 37748736 | tf_op jit(solution)/shard_map/vmap()/dot_general | solution.py:21
  212.4 17.6 %copy.62 = f32[16,512,512]{1,2,0:T(8,128)} copy(f32[16,512,512]{2,1,0:T(8,128)} %convolution_add_fusion) | data formatting | bytes 33554432 | tf_op jit(solution)/shard_map/vmap()/add | solution.py:22
  230.0 15.1 %fusion.5 = bf16[16,512,512]{2,1,0:T(8,128)(2,1)} fusion(f32[16,512,512]{2,1,0:T(8,128)} %convolution_add_fusion, f32[16,512,512]{1,2,0:T(8,128)} %copy.62), kind=kLoop, calls=%fused_computation.22 | loop fusion | flops 8388608 | bytes 41943040 | tf_op jit(solution)/shard_map/vmap()/convert_element_type | solution.py:23
  245.0 21.2 %reshape.134 = bf16[16,8,64,8,64]{4,3,2,1,0:T(8,128)(2,1)} reshape(bf16[16,512,512]{2,1,0:T(8,128)(2,1)} %fusion.5) | data formatting | bytes 16777216 | tf_op jit(solution)/shard_map/vmap()/reshape | solution.py:24
  266.3 15.1 %copy.93 = bf16[16,8,64,8,64]{4,2,3,1,0:T(8,128)(2,1)} copy(bf16[16,8,64,8,64]{4,3,2,1,0:T(8,128)(2,1)} %reshape.134) | data formatting | bytes 16777216 | tf_op jit(solution)/shard_map/vmap()/reshape | solution.py:24
  281.3 22.6 %reshape.135 = bf16[16,64,4096]{2,1,0:T(8,128)(2,1)} reshape(bf16[16,8,8,64,64]{4,3,2,1,0:T(8,128)(2,1)} %bitcast.160) | data formatting | bytes 16777216 | tf_op jit(solution)/shard_map/vmap()/reshape | solution.py:25
  303.9 11.2 %copy.64 = bf16[16,64,4096]{2,0,1:T(8,128)(2,1)} copy(bf16[16,64,4096]{2,1,0:T(8,128)(2,1)} %reshape.135) | data formatting | bytes 16777216 | tf_op jit(solution)/shard_map/vmap()/reshape | solution.py:25
  315.2 9.5 gather_fusion
  324.7 7.6 select_bitcast_fusion
  332.3 7.8 copy.65
  340.1 7.4 all-to-all-start.1
  347.7 28.5 %gather_fusion.1 = bf16[512,16,4096]{2,1,0:T(8,128)(2,1)} fusion(bf16[16,64,4096]{2,0,1:T(8,128)(2,1)} %copy.64, s32[1024]{0:T(1024)S(1)} %pad_clamp_fusion), kind=kCustom, calls=%fused_computation.1 | custom fusion | bytes 134219776 | tf_op jit(solution)/shard_map/jit(_take)/gather | solution.py:50
  376.2 30.4 %fusion = f32[512,1,16]{2,1,0:T(1,128)S(1)} fusion(bf16[512,16,4096]{2,1,0:T(8,128)(2,1)} %gather_fusion.1, pred[512]{0:T(512)(128)(4,1)S(1)} %compare_and_fusion, bf16[512,4096,1]{1,0,2:T(8,128)(2,1)} %bitcast.170), kind=kOutput, calls=%fused_computation.16 | convolution fusion | flops 100663296 | bytes 71336448 | tf_op jit(solution)/shard_map/if,nif->in/dot_general | solution.py:51
  408.1 9.1 reduce-window.6
  417.9 7.1 scatter_custom_fusion
  425.7 108.3 %all-to-all-done.1 = bf16[16,2,32,4096]{3,0,1,2:T(8,128)(2,1)} async-done(((bf16[16,2,32,4096]{3,0,1,2:T(8,128)(2,1)}), bf16[16,2,32,4096]{3,0,1,2:T(8,128)(2,1)}, u32[]{:S(2)}, u32[]{:S(2)}) %all-to-all-start.1) | async-done | bytes 8388640 | tf_op jit(solution)/shard_map/all_to_all | solution.py:58
  534.0 8.5 all-to-all-start
  542.5 5.2 fusion.68
  547.8 15.3 %fusion.6 = f32[16,32,1792]{2,1,0:T(8,128)} fusion(bf16[1792,4096]{1,0:T(8,128)(2,1)} %param.15, bf16[16,1,32,4096]{3,0,1,2:T(8,128)(2,1)S(1)} %get-tuple-element.97), kind=kOutput, calls=%fused_computation.24 | convolution fusion | flops 7516192768 | bytes 22544384 | tf_op jit(solution)/shard_map/sf,ndf->sdn/dot_general | solution.py:61
  563.0 18.1 %select_bitcast_fusion.1 = f32[1792,32,16]{0,1,2:T(8,128)} fusion(f32[16,32,1792]{2,1,0:T(8,128)} %fusion.6, bf16[1792,4096]{1,0:T(8,128)(2,1)} %param.15, bf16[16,1,32,4096]{3,0,1,2:T(8,128)(2,1)} %get-tuple-element.96, pred[1792]{0:T(1024)(128)(4,1)S(1)} %get-tuple-element.109, pred[1792]{0:T(1024)(128)(4,1)S(1)} %get-tuple-element.108), kind=kOutput, calls=%fused_computation.34 | convolution fusion | flops 7518027776 | bytes 26217984 | tf_op jit(solution)/shard_map/sf,ndf->sdn/dot_general | solution.py:61
  581.1 6.0 copy.68
  587.1 5.1 copy.69
  592.2 13.1 %scatter_custom_fusion.1 = f32[1792,512]{1,0:T(8,128)} fusion(s32[1792]{0:T(1024)S(1)} %compare_select_fusion.1, f32[1792,512]{1,0:T(8,128)} %copy.69, f32[]{:T(128)} %constant.245.clone.1), kind=kCustom, calls=%fused_computation.36 | custom fusion | bytes 3670528 | tf_op jit(solution)/shard_map/scatter | solution.py:81
  605.4 6.1 all-to-all-start.2
  615.8 4.9 gather_fusion.2
  622.6 11.7 %cholesky.103 = f32[128,128]{1,0:T(8,128)S(1)} custom-call(f32[128,128]{1,0:T(8,128)S(1)} %cholesky.263), custom_call_target="Cholesky" | custom-call | tf_op jit(solution)/shard_map/jit(cholesky)/cholesky | solution.py:55
  634.5 9.8 custom-call.30
  645.0 11.7 %cholesky.215 = f32[128,128]{1,0:T(8,128)S(1)} custom-call(f32[128,128]{1,0:T(8,128)S(1)} %cholesky.267), custom_call_target="Cholesky" | custom-call | tf_op jit(solution)/shard_map/jit(cholesky)/cholesky | solution.py:55
  656.7 10.0 %custom-call.31 = f32[1,128,128]{1,2,0:T(8,128)S(1)} custom-call(f32[1,128,128]{2,1,0:T(8,128)S(1)} %get-tuple-element.104), custom_call_target="InvertDiagBlocksLowerTriangular" | custom-call | tf_op jit(solution)/shard_map/jit(cholesky)/cholesky | solution.py:55
  667.4 11.7 %cholesky.236 = f32[128,128]{1,0:T(8,128)S(1)} custom-call(f32[128,128]{1,0:T(8,128)S(1)} %cholesky.272), custom_call_target="Cholesky" | custom-call | tf_op jit(solution)/shard_map/jit(cholesky)/cholesky | solution.py:55
  679.1 9.8 custom-call.32
  689.5 11.7 %cholesky.253 = f32[128,128]{1,0:T(8,128)S(1)} custom-call(f32[128,128]{1,0:T(8,128)S(1)} %convolution_subtract_fusion.5), custom_call_target="Cholesky" | custom-call | tf_op jit(solution)/shard_map/jit(cholesky)/cholesky | solution.py:55
  706.6 10.6 %while.9 = (s32[]{:T(128)}, f32[512,512]{1,0:T(8,128)S(1)}, s32[4,2]{0,1:T(2,128)S(1)}, f32[4,128,128]{2,1,0:T(8,128)}, s32[]{:T(128)}) while((s32[]{:T(128)}, f32[512,512]{1,0:T(8,128)S(1)}, s32[4,2]{0,1:T(2,128)S(1)}, f32[4,128,128]{2,1,0:T(8,128)}, s32[]{:T(128)}) %tuple.99), condition=%wide.while_cond.4, body=%wide.while_body.4.sunk | while | flops 2 | bytes 132705 | solution.py:109
  717.2 40.1 %custom-call.33 = f32[4,128,128]{1,2,0:T(8,128)S(1)} custom-call(f32[4,128,128]{2,1,0:T(8,128)} %get-tuple-element.41), custom_call_target="InvertDiagBlocksLowerTriangular" | custom-call | tf_op jit(solution)/shard_map/triangular_solve | solution.py:109
  757.4 11.6 %scatter_custom_fusion.2 = f32[1024,512]{1,0:T(8,128)S(1)} fusion(s32[1792]{0:T(1024)S(1)} %fusion.57, f32[1792,512]{1,0:T(8,128)} %bitcast.17, f32[]{:T(128)} %constant.245.clone.1), kind=kCustom, calls=%fused_computation.63 | custom fusion | bytes 2097664 | tf_op jit(solution)/shard_map/scatter | solution.py:107
  773.7 2.8 fusion.21
  779.0 150.6 %all-gather.6.cloned.1.call-done = f32[4096,512]{0,1:T(8,128)} async-done(((f32[1024,512]{0,1:T(8,128)}), f32[4096,512]{0,1:T(8,128)}) %all-gather.6.cloned.1.call-update) | async-done | bytes 8388624 | tf_op jit(solution)/shard_map/all_gather | solution.py:112
  933.4 20.4 %all-gather.8.cloned.1.call-done = f32[512,512]{1,0:T(8,128)} async-done(((f32[64,512]{1,0:T(8,128)}), f32[512,512]{1,0:T(8,128)}) %all-gather.8.cloned.1.call-update) | async-done | bytes 1048592 | tf_op jit(solution)/shard_map/all_gather | solution.py:115
  953.7 31.8 %convolution_subtract_fusion = f32[4096,512]{1,0:T(8,128)} fusion(f32[4096,512]{1,0:T(8,128)} %param.19, f32[4096,512]{0,1:T(8,128)} %all-gather.6.cloned.1.call-done, f32[512,512]{1,0:T(8,128)} %all-gather.8.cloned.1.call-done), kind=kOutput, calls=%fused_computation.31 | convolution fusion | flops 12886999040 | bytes 26214400 | tf_op jit(solution)/shard_map/dot_general | solution.py:116
  (286 shorter events, 152.7 us)
Async XLA Ops:
  7.2 5.5 copy-start.5
  80.8 38.0 %copy-start.3 = (f32[16,64,512]{2,1,0:T(8,128)}, f32[16,64,512]{2,1,0:T(8,128)S(1)}, u32[]{:S(2)}) copy-start(f32[16,64,512]{2,1,0:T(8,128)S(1)} %get-tuple-element.17) | copy-start | bytes 6291460
  118.7 5.0 copy-start.1
  176.4 17.1 %copy-start.2 = (f32[16,512,64]{1,2,0:T(8,128)S(1)}, f32[16,512,64]{1,2,0:T(8,128)}, u32[]{:S(2)}) copy-start(f32[16,512,64]{1,2,0:T(8,128)} %fusion.73) | copy-start | bytes 6291460
  176.4 17.1 %copy-start.4 = (f32[16,64,512]{2,1,0:T(8,128)S(1)}, f32[16,64,512]{2,1,0:T(8,128)}, u32[]{:S(2)}) copy-start(f32[16,64,512]{2,1,0:T(8,128)} %get-tuple-element.33) | copy-start | bytes 6291460
  340.1 7.5 copy-start.6
  340.1 193.9 %all-to-all-start.1 = ((bf16[16,2,32,4096]{3,0,1,2:T(8,128)(2,1)}), bf16[16,2,32,4096]{3,0,1,2:T(8,128)(2,1)}, u32[]{:S(2)}, u32[]{:S(2)}) async-start(bf16[16,2,32,4096]{3,0,1,2:T(8,128)(2,1)} %copy.65), calls=%async_computation.1 | async-start | bytes 16777216 | tf_op jit(solution)/shard_map/all_to_all | solution.py:58
  347.6 265.2 %all-gather.4.cloned.1.call-start = ((), (), s32[]{:S(2)}) async-start(), calls=%async_computation.3 | async-start | bytes 1081344 | tf_op jit(solution)/shard_map/all_gather | solution.py:52
  376.2 31.8 %copy-start.7 = (s32[1792]{0:T(1024)S(1)}, s32[1792]{0:T(1024)}, u32[]{:S(2)}) copy-start(s32[1792]{0:T(1024)} %param.17) | copy-start | bytes 21508
  376.2 49.5 %copy-start.8 = (s32[1792]{0:T(1024)S(1)}, s32[1792]{0:T(1024)}, u32[]{:S(2)}) copy-start(s32[1792]{0:T(1024)} %param.16) | copy-start | bytes 21508
  534.0 71.4 %all-to-all-start = ((s32[32,1,56]{2,1,0:T(1,128)}), s32[32,1,56]{2,1,0:T(1,128)S(1)}, u32[]{:S(2)}, u32[]{:S(2)}) async-start(s32[32,1,56]{2,1,0:T(1,128)} %all_to_all.12), calls=%async_computation | async-start | bytes 32768 | tf_op jit(solution)/shard_map/all_to_all | solution.py:96
  605.4 152.0 %all-to-all-start.2 = ((f32[32,56,512]{2,1,0:T(8,128)}), f32[32,56,512]{2,1,0:T(8,128)}, u32[]{:S(2)}, u32[]{:S(2)}) async-start(f32[32,56,512]{2,1,0:T(8,128)} %bitcast.164), calls=%async_computation.2 | async-start | bytes 7340032 | tf_op jit(solution)/shard_map/all_to_all | solution.py:89
  611.4 318.2 %all-gather.6.cloned.1.call-start = ((), (), s32[]{:S(2)}) async-start(), calls=%async_computation.4 | async-start | bytes 10485760 | tf_op jit(solution)/shard_map/all_gather | solution.py:112
  778.7 152.8 %copy-start = (f32[1024,512]{0,1:T(8,128)S(1)}, f32[1024,512]{0,1:T(8,128)}, u32[]{:S(2)}) copy-start(f32[1024,512]{0,1:T(8,128)} %pad_maximum_fusion) | copy-start | bytes 6291460
  778.7 175.0 %all-gather.8.cloned.1.call-start = ((), (), s32[]{:S(2)}) async-start(), calls=%async_computation.5 | async-start | bytes 1179648 | tf_op jit(solution)/shard_map/all_gather | solution.py:115
Sparse Core Ops, SparseCore 0:
  407.5 96.1 all-gather.3
  778.8 150.7 all-gather.5
  932.1 21.5 all-gather.7
where the time goes:
time: 1000 us; the launch traced here: 992 us
  local copies, waits for them, and re-layouts  362 us (36%)
  waiting for transfers between devices  279 us (28%)
  other arithmetic  159 us (16%)
  matrix products  151 us (15%)
  starting transfers between devices  22.4 us (2%)
  between operations  18.5 us (2%)
    all_gather x1, waiting for transfers between devices, body(): all_rows = lax.all_gather(lower_slab, 'col', axis=0, tiled=True)  151 us
    gather x192, local copies, waits for them, and re-layouts  149 us
    all_to_all x1, waiting for transfers between devices, body(): lax.all_to_all(outgoing, ('row', 'col'), split_axis=2, concat_axis=2, til...  108 us
    another operation x15, other arithmetic, body(): jnp.linalg.cholesky(symmetric + diag_shift * jnp.eye(panel_cols, dtype=jn...  79.2 us
    another operation x4, other arithmetic, body(): lax.linalg.triangular_solve(factor, row_slab, left_side=False, lower=True...  41.8 us
    reshape x2, local copies, waits for them, and re-layouts, build_h(): h_mat.reshape(block_count, block_size, block_count, block_size)  36.3 us
    reshape x2, local copies, waits for them, and re-layouts, build_h(): return h_mat.reshape(block_count * block_count, block_size * block_size)  33.7 us
    dot_general x2, matrix products, body(): jnp.einsum('sf,ndf->sdn', cons_blocks, received[:, slot_index], preferred...  33.3 us
  transfers between devices with their start and end apart: 6, of which 3 were waited for; matrix products, arithmetic and copies ran while one was open for 29% of the time, Pallas kernels for 0%

commit v1 on v0

--- a/solution.py
+++ b/solution.py
@@ -109,7 +109,14 @@
     lower_slab = lax.linalg.triangular_solve(
         factor, row_slab, left_side=False, lower=True, transpose_a=True
     )
-    all_rows = lax.all_gather(lower_slab, "col", axis=0, tiled=True)
+    ways, here = (lax.axis_size("col"), lax.axis_index("col"))
+    all_rows, reach = (lower_slab, 1)
+    while reach < ways:
+        theirs = lax.ppermute(all_rows, "col", [(d, d ^ reach) for d in range(ways)])
+        mine_first = jnp.concatenate([all_rows, theirs], axis=0)
+        theirs_first = jnp.concatenate([theirs, all_rows], axis=0)
+        all_rows = jnp.where(here & reach == 0, mine_first, theirs_first)
+        reach = 2 * reach
     block_rows = trailing.shape[1] // rows_size
     own_rows = lax.dynamic_slice_in_dim(all_rows, col_index * block_rows, block_rows, 0)
     picked = lax.all_gather(own_rows, "row", axis=0, tiled=True)

time: 1000 us -> 1100 us (1.10)
  waiting for transfers between devices: 279 us -> 358 us
  other arithmetic: 159 us -> 172 us
    ppermute x0 -> x2, waiting for transfers between devices: none -> 226 us  [body(): lax.ppermute(all_rows, 'col', [(d, d ^ reach) for d in range(ways)])]
    all_gather x1 -> x0, waiting for transfers between devices: 151 us -> none  [body(): all_rows = lax.all_gather(lower_slab, 'col', axis=0, tiled=True)]
    select_n x0 -> x2, other arithmetic: none -> 14.3 us  [body(): all_rows = jnp.where(here & reach == 0, mine_first, theirs_first)]
  transfers between devices with their start and end apart: 6 -> 7, of which waited for: 3 -> 4; matrix products, arithmetic and copies ran while one was open for 29% -> 26% of each run, Pallas kernels for 0% -> 0%
where the time goes in v1:
time: 1100 us; the launch traced here: 1090 us
  local copies, waits for them, and re-layouts  364 us (33%)
  waiting for transfers between devices  358 us (33%)
  other arithmetic  172 us (16%)
  matrix products  154 us (14%)
  starting transfers between devices  26.6 us (2%)
  between operations  18.8 us (2%)
    ppermute x2, waiting for transfers between devices, body(): lax.ppermute(all_rows, 'col', [(d, d ^ reach) for d in range(ways)])  226 us
    gather x192, local copies, waits for them, and re-layouts  149 us
    all_to_all x1, waiting for transfers between devices, body(): lax.all_to_all(outgoing, ('row', 'col'), split_axis=2, concat_axis=2, til...  108 us
    another operation x15, other arithmetic, body(): jnp.linalg.cholesky(symmetric + diag_shift * jnp.eye(panel_cols, dtype=jn...  79.3 us
    another operation x4, other arithmetic, body(): lax.linalg.triangular_solve(factor, row_slab, left_side=False, lower=True...  40.5 us
    reshape x2, local copies, waits for them, and re-layouts, build_h(): h_mat.reshape(block_count, block_size, block_count, block_size)  36.3 us
    reshape x2, local copies, waits for them, and re-layouts, build_h(): return h_mat.reshape(block_count * block_count, block_size * block_size)  33.7 us
    dot_general x2, matrix products, body(): jnp.einsum('sf,ndf->sdn', cons_blocks, received[:, slot_index], preferred...  33.3 us
  transfers between devices with their start and end apart: 7, of which 4 were waited for; matrix products, arithmetic and copies ran while one was open for 26% of the time, Pallas kernels for 0%

profile of v1, /device:TPU:0, one launch (start us, length us, event | category | flops | bytes accessed | tf_op | source)
XLA Modules:
  0.0 1093.4 jit_solution(9905842228860316831)
XLA Ops:
  10.2 2.5 broadcast.301.clone
  12.6 31.8 %while.5 = (s32[]{:T(128)}, f32[512,512]{1,0:T(8,128)S(1)}, s32[16,2]{0,1:T(2,128)S(1)}, f32[16,512,64]{2,1,0:T(8,128)}, s32[]{:T(128)}) while((s32[]{:T(128)}, f32[512,512]{1,0:T(8,128)S(1)}, s32[16,2]{0,1:T(2,128)S(1)}, f32[16,512,64]{2,1,0:T(8,128)}, s32[]{:T(128)}) %tuple.106), condition=%wide.while_cond, body=%wide.while_body.sunk | while | flops 2 | bytes 394329 | solution.py:16
  45.8 34.9 %while.6 = (s32[]{:T(128)}, f32[512,512]{1,0:T(8,128)}, s32[16,2]{0,1:T(2,128)S(1)}, f32[16,64,512]{2,1,0:T(8,128)S(1)}, s32[]{:T(128)}) while((s32[]{:T(128)}, f32[512,512]{1,0:T(8,128)}, s32[16,2]{0,1:T(2,128)S(1)}, f32[16,64,512]{2,1,0:T(8,128)S(1)}, s32[]{:T(128)}) %tuple.90), condition=%wide.while_cond.1, body=%wide.while_body.1.sunk | while | flops 2 | bytes 262241 | solution.py:18
  80.8 2.6 broadcast.301.clone.1
  83.4 35.3 %while.7 = (s32[]{:T(128)}, f32[512,512]{1,0:T(8,128)S(1)}, s32[16,2]{0,1:T(2,128)S(1)}, f32[16,512,64]{2,1,0:T(8,128)}, s32[]{:T(128)}) while((s32[]{:T(128)}, f32[512,512]{1,0:T(8,128)S(1)}, s32[16,2]{0,1:T(2,128)S(1)}, f32[16,512,64]{2,1,0:T(8,128)}, s32[]{:T(128)}) %tuple.107), condition=%wide.while_cond.2, body=%wide.while_body.2.sunk | while | flops 2 | bytes 394329 | solution.py:17
  118.7 5.0 fusion.71
  123.8 4.1 fusion.73
  129.4 47.0 %while.8 = (s32[]{:T(128)}, f32[512,512]{1,0:T(8,128)}, s32[16,2]{0,1:T(2,128)S(1)}, f32[16,64,512]{2,1,0:T(8,128)}, s32[]{:T(128)}) while((s32[]{:T(128)}, f32[512,512]{1,0:T(8,128)}, s32[16,2]{0,1:T(2,128)S(1)}, f32[16,64,512]{2,1,0:T(8,128)}, s32[]{:T(128)}) %tuple.108), condition=%wide.while_cond.3, body=%wide.while_body.3.sunk | while | flops 2 | bytes 263257 | solution.py:19
  133.0 2.3 bitcast_dynamic-update-slice_fusion.13
  136.0 2.3 bitcast_dynamic-update-slice_fusion.13
  138.9 2.3 bitcast_dynamic-update-slice_fusion.13
  141.9 2.3 bitcast_dynamic-update-slice_fusion.13
  147.7 2.3 bitcast_dynamic-update-slice_fusion.13
  150.6 2.3 bitcast_dynamic-update-slice_fusion.13
  156.5 2.3 bitcast_dynamic-update-slice_fusion.13
  159.5 2.3 bitcast_dynamic-update-slice_fusion.13
  162.4 2.3 bitcast_dynamic-update-slice_fusion.13
  174.1 2.3 bitcast_dynamic-update-slice_fusion.13
  176.4 17.1 %fusion.72 = f32[16,512,512]{2,1,0:T(8,128)} fusion(f32[16,512,64]{1,2,0:T(8,128)S(1)} %fusion.71, f32[16,64,512]{2,1,0:T(8,128)} %copy-done.3), kind=kOutput, calls=%fused_computation.162 | convolution fusion | flops 3221225472 | bytes 20971520 | tf_op jit(solution)/shard_map/vmap()/dot_general | solution.py:20
  193.5 19.1 %convolution_add_fusion = f32[16,512,512]{2,1,0:T(8,128)} fusion(f32[16,512,512]{2,1,0:T(8,128)} %fusion.72, f32[16,512,64]{1,2,0:T(8,128)S(1)} %copy-done.2, f32[16,64,512]{2,1,0:T(8,128)S(1)} %copy-done.4), kind=kOutput, calls=%fused_computation.28 | convolution fusion | flops 3225419776 | bytes 37748736 | tf_op jit(solution)/shard_map/vmap()/dot_general | solution.py:21
  212.6 17.6 %copy.62 = f32[16,512,512]{1,2,0:T(8,128)} copy(f32[16,512,512]{2,1,0:T(8,128)} %convolution_add_fusion) | data formatting | bytes 33554432 | tf_op jit(solution)/shard_map/vmap()/add | solution.py:22
  230.2 15.1 %fusion.5 = bf16[16,512,512]{2,1,0:T(8,128)(2,1)} fusion(f32[16,512,512]{2,1,0:T(8,128)} %convolution_add_fusion, f32[16,512,512]{1,2,0:T(8,128)} %copy.62), kind=kLoop, calls=%fused_computation.22 | loop fusion | flops 8388608 | bytes 41943040 | tf_op jit(solution)/shard_map/vmap()/convert_element_type | solution.py:23
  245.3 21.2 %reshape.134 = bf16[16,8,64,8,64]{4,3,2,1,0:T(8,128)(2,1)} reshape(bf16[16,512,512]{2,1,0:T(8,128)(2,1)} %fusion.5) | data formatting | bytes 16777216 | tf_op jit(solution)/shard_map/vmap()/reshape | solution.py:24
  266.5 15.1 %copy.93 = bf16[16,8,64,8,64]{4,2,3,1,0:T(8,128)(2,1)} copy(bf16[16,8,64,8,64]{4,3,2,1,0:T(8,128)(2,1)} %reshape.134) | data formatting | bytes 16777216 | tf_op jit(solution)/shard_map/vmap()/reshape | solution.py:24
  281.6 22.6 %reshape.135 = bf16[16,64,4096]{2,1,0:T(8,128)(2,1)} reshape(bf16[16,8,8,64,64]{4,3,2,1,0:T(8,128)(2,1)} %bitcast.160) | data formatting | bytes 16777216 | tf_op jit(solution)/shard_map/vmap()/reshape | solution.py:25
  304.1 11.2 %copy.64 = bf16[16,64,4096]{2,0,1:T(8,128)(2,1)} copy(bf16[16,64,4096]{2,1,0:T(8,128)(2,1)} %reshape.135) | data formatting | bytes 16777216 | tf_op jit(solution)/shard_map/vmap()/reshape | solution.py:25
  315.4 9.3 gather_fusion
  324.7 7.6 select_bitcast_fusion
  332.3 7.8 copy.65
  340.1 7.5 all-to-all-start.1
  347.6 28.5 %gather_fusion.1 = bf16[512,16,4096]{2,1,0:T(8,128)(2,1)} fusion(bf16[16,64,4096]{2,0,1:T(8,128)(2,1)} %copy.64, s32[1024]{0:T(1024)S(1)} %pad_clamp_fusion), kind=kCustom, calls=%fused_computation.1 | custom fusion | bytes 134219776 | tf_op jit(solution)/shard_map/jit(_take)/gather | solution.py:50
  376.2 30.4 %fusion = f32[512,1,16]{2,1,0:T(1,128)S(1)} fusion(bf16[512,16,4096]{2,1,0:T(8,128)(2,1)} %gather_fusion.1, pred[512]{0:T(512)(128)(4,1)S(1)} %compare_and_fusion, bf16[512,4096,1]{1,0,2:T(8,128)(2,1)} %bitcast.170), kind=kOutput, calls=%fused_computation.16 | convolution fusion | flops 100663296 | bytes 71336448 | tf_op jit(solution)/shard_map/if,nif->in/dot_general | solution.py:51
  408.1 9.1 reduce-window.6
  417.9 7.1 scatter_custom_fusion
  425.7 108.3 %all-to-all-done.1 = bf16[16,2,32,4096]{3,0,1,2:T(8,128)(2,1)} async-done(((bf16[16,2,32,4096]{3,0,1,2:T(8,128)(2,1)}), bf16[16,2,32,4096]{3,0,1,2:T(8,128)(2,1)}, u32[]{:S(2)}, u32[]{:S(2)}) %all-to-all-start.1) | async-done | bytes 8388640 | tf_op jit(solution)/shard_map/all_to_all | solution.py:58
  534.0 8.8 all-to-all-start
  542.8 5.2 fusion.68
  548.0 15.3 %fusion.6 = f32[16,32,1792]{2,1,0:T(8,128)} fusion(bf16[1792,4096]{1,0:T(8,128)(2,1)} %param.15, bf16[16,1,32,4096]{3,0,1,2:T(8,128)(2,1)S(1)} %get-tuple-element.97), kind=kOutput, calls=%fused_computation.24 | convolution fusion | flops 7516192768 | bytes 22544384 | tf_op jit(solution)/shard_map/sf,ndf->sdn/dot_general | solution.py:61
  563.2 18.1 %select_bitcast_fusion.1 = f32[1792,32,16]{0,1,2:T(8,128)} fusion(f32[16,32,1792]{2,1,0:T(8,128)} %fusion.6, bf16[1792,4096]{1,0:T(8,128)(2,1)} %param.15, bf16[16,1,32,4096]{3,0,1,2:T(8,128)(2,1)} %get-tuple-element.96, pred[1792]{0:T(1024)(128)(4,1)S(1)} %get-tuple-element.109, pred[1792]{0:T(1024)(128)(4,1)S(1)} %get-tuple-element.108), kind=kOutput, calls=%fused_computation.36 | convolution fusion | flops 7518027776 | bytes 26217984 | tf_op jit(solution)/shard_map/sf,ndf->sdn/dot_general | solution.py:61
  581.3 6.0 copy.68
  587.3 5.1 copy.69
  592.4 13.1 %scatter_custom_fusion.1 = f32[1792,512]{1,0:T(8,128)} fusion(s32[1792]{0:T(1024)S(1)} %compare_select_fusion.1, f32[1792,512]{1,0:T(8,128)} %copy.69, f32[]{:T(128)} %constant.247.clone.1), kind=kCustom, calls=%fused_computation.38 | custom fusion | bytes 3670528 | tf_op jit(solution)/shard_map/scatter | solution.py:81
  605.6 6.1 all-to-all-start.2
  616.1 4.7 gather_fusion.2
  622.8 11.7 %cholesky.103 = f32[128,128]{1,0:T(8,128)S(1)} custom-call(f32[128,128]{1,0:T(8,128)S(1)} %cholesky.263), custom_call_target="Cholesky" | custom-call | tf_op jit(solution)/shard_map/jit(cholesky)/cholesky | solution.py:55
  634.7 9.8 custom-call.30
  645.2 11.7 %cholesky.215 = f32[128,128]{1,0:T(8,128)S(1)} custom-call(f32[128,128]{1,0:T(8,128)S(1)} %cholesky.267), custom_call_target="Cholesky" | custom-call | tf_op jit(solution)/shard_map/jit(cholesky)/cholesky | solution.py:55
  656.9 10.2 custom-call.31
  667.8 11.7 %cholesky.236 = f32[128,128]{1,0:T(8,128)S(1)} custom-call(f32[128,128]{1,0:T(8,128)S(1)} %cholesky.272), custom_call_target="Cholesky" | custom-call | tf_op jit(solution)/shard_map/jit(cholesky)/cholesky | solution.py:55
  679.5 9.8 custom-call.32
  690.0 11.7 %cholesky.253 = f32[128,128]{1,0:T(8,128)S(1)} custom-call(f32[128,128]{1,0:T(8,128)S(1)} %convolution_subtract_fusion.5), custom_call_target="Cholesky" | custom-call | tf_op jit(solution)/shard_map/jit(cholesky)/cholesky | solution.py:55
  707.1 10.1 while.9
  717.1 40.2 %custom-call.33 = f32[4,128,128]{1,2,0:T(8,128)S(1)} custom-call(f32[4,128,128]{2,1,0:T(8,128)} %get-tuple-element.41), custom_call_target="InvertDiagBlocksLowerTriangular" | custom-call | tf_op jit(solution)/shard_map/triangular_solve | solution.py:109
  757.3 11.6 %scatter_custom_fusion.2 = f32[1024,512]{1,0:T(8,128)S(1)} fusion(s32[1792]{0:T(1024)S(1)} %fusion.57, f32[1792,512]{1,0:T(8,128)} %bitcast.17, f32[]{:T(128)} %constant.247.clone.1), kind=kCustom, calls=%fused_computation.65 | custom fusion | bytes 2097664 | tf_op jit(solution)/shard_map/scatter | solution.py:107
  772.1 2.7 convolution_subtract_fusion.1
  775.4 3.8 fusion.21
  782.4 46.1 %collective-permute-done = f32[1024,512]{0,1:T(8,128)} collective-permute-done((f32[1024,512]{0,1:T(8,128)S(1)}, f32[1024,512]{0,1:T(8,128)}, u32[]{:S(2)}, u32[]{:S(2)}) %collective-permute-start) | collective-permute-done | bytes 2097184 | tf_op jit(solution)/shard_map/ppermute | solution.py:115
  828.5 7.3 maximum_select_fusion.1
  835.8 2.5 collective-permute-start.1
  838.4 180.4 %collective-permute-done.1 = f32[2048,512]{0,1:T(8,128)} collective-permute-done((f32[2048,512]{0,1:T(8,128)}, f32[2048,512]{0,1:T(8,128)}, u32[]{:S(2)}, u32[]{:S(2)}) %collective-permute-start.1) | collective-permute-done | bytes 4194336 | tf_op jit(solution)/shard_map/ppermute | solution.py:115
  1018.7 6.9 maximum_select_fusion
  1025.7 3.2 copy-done
  1031.7 22.7 %all-gather.5.cloned.1.call-done = f32[512,512]{1,0:T(8,128)} async-done(((f32[64,512]{1,0:T(8,128)}), f32[512,512]{1,0:T(8,128)}) %all-gather.5.cloned.1.call-update) | async-done | bytes 1048592 | tf_op jit(solution)/shard_map/all_gather | solution.py:122
  1054.3 32.0 %convolution_subtract_fusion = f32[4096,512]{1,0:T(8,128)} fusion(f32[4096,512]{1,0:T(8,128)} %param.19, f32[4096,512]{0,1:T(8,128)} %copy-done, f32[512,512]{1,0:T(8,128)} %all-gather.5.cloned.1.call-done), kind=kOutput, calls=%fused_computation.32 | convolution fusion | flops 12886999040 | bytes 26214400 | tf_op jit(solution)/shard_map/dot_general | solution.py:123
  (295 shorter events, 164.4 us)
Async XLA Ops:
  7.2 5.5 copy-start.6
  80.8 38.0 %copy-start.3 = (f32[16,64,512]{2,1,0:T(8,128)}, f32[16,64,512]{2,1,0:T(8,128)S(1)}, u32[]{:S(2)}) copy-start(f32[16,64,512]{2,1,0:T(8,128)S(1)} %get-tuple-element.17) | copy-start | bytes 6291460
  118.7 5.0 copy-start.1
  176.4 17.1 %copy-start.2 = (f32[16,512,64]{1,2,0:T(8,128)S(1)}, f32[16,512,64]{1,2,0:T(8,128)}, u32[]{:S(2)}) copy-start(f32[16,512,64]{1,2,0:T(8,128)} %fusion.73) | copy-start | bytes 6291460
  176.4 17.1 %copy-start.4 = (f32[16,64,512]{2,1,0:T(8,128)S(1)}, f32[16,64,512]{2,1,0:T(8,128)}, u32[]{:S(2)}) copy-start(f32[16,64,512]{2,1,0:T(8,128)} %get-tuple-element.33) | copy-start | bytes 6291460
  340.1 7.5 copy-start.9
  340.1 193.9 %all-to-all-start.1 = ((bf16[16,2,32,4096]{3,0,1,2:T(8,128)(2,1)}), bf16[16,2,32,4096]{3,0,1,2:T(8,128)(2,1)}, u32[]{:S(2)}, u32[]{:S(2)}) async-start(bf16[16,2,32,4096]{3,0,1,2:T(8,128)(2,1)} %copy.65), calls=%async_computation.1 | async-start | bytes 16777216 | tf_op jit(solution)/shard_map/all_to_all | solution.py:58
  347.5 265.6 %all-gather.3.cloned.1.call-start = ((), (), s32[]{:S(2)}) async-start(), calls=%async_computation.3 | async-start | bytes 1081344 | tf_op jit(solution)/shard_map/all_gather | solution.py:52
  376.2 31.8 %copy-start.10 = (s32[1792]{0:T(1024)S(1)}, s32[1792]{0:T(1024)}, u32[]{:S(2)}) copy-start(s32[1792]{0:T(1024)} %param.17) | copy-start | bytes 21508
  376.2 49.5 %copy-start.11 = (s32[1792]{0:T(1024)S(1)}, s32[1792]{0:T(1024)}, u32[]{:S(2)}) copy-start(s32[1792]{0:T(1024)} %param.16) | copy-start | bytes 21508
  534.0 71.6 %all-to-all-start = ((s32[32,1,56]{2,1,0:T(1,128)}), s32[32,1,56]{2,1,0:T(1,128)S(1)}, u32[]{:S(2)}, u32[]{:S(2)}) async-start(s32[32,1,56]{2,1,0:T(1,128)} %all_to_all.12), calls=%async_computation | async-start | bytes 32768 | tf_op jit(solution)/shard_map/all_to_all | solution.py:96
  605.6 151.7 %all-to-all-start.2 = ((f32[32,56,512]{2,1,0:T(8,128)}), f32[32,56,512]{2,1,0:T(8,128)}, u32[]{:S(2)}, u32[]{:S(2)}) async-start(f32[32,56,512]{2,1,0:T(8,128)} %bitcast.164), calls=%async_computation.2 | async-start | bytes 7340032 | tf_op jit(solution)/shard_map/all_to_all | solution.py:89
  611.6 442.7 %all-gather.5.cloned.1.call-start = ((), (), s32[]{:S(2)}) async-start(), calls=%async_computation.4 | async-start | bytes 1179648 | tf_op jit(solution)/shard_map/all_gather | solution.py:122
  717.1 40.2 %copy-start.8 = (f32[512,512]{1,0:T(8,128)}, f32[512,512]{1,0:T(8,128)S(1)}, u32[]{:S(2)}) copy-start(f32[512,512]{1,0:T(8,128)S(1)} %get-tuple-element.333) | copy-start | bytes 3145732
  775.4 4.5 copy-start.5
  779.9 0.8 copy-start.7
  780.7 47.8 %collective-permute-start = (f32[1024,512]{0,1:T(8,128)S(1)}, f32[1024,512]{0,1:T(8,128)}, u32[]{:S(2)}, u32[]{:S(2)}) collective-permute-start(f32[1024,512]{0,1:T(8,128)S(1)} %pad_maximum_fusion), channel_id=1, source_target_pairs={{0,1},{1,0},{2,3},{3,2},{4,5},{5,4},{6,7},{7,6},{8,9},{9,8},{10,11... | collective-permute-start | bytes 6291464 | tf_op jit(solution)/shard_map/ppermute | solution.py:115
  835.8 182.9 %collective-permute-start.1 = (f32[2048,512]{0,1:T(8,128)}, f32[2048,512]{0,1:T(8,128)}, u32[]{:S(2)}, u32[]{:S(2)}) collective-permute-start(f32[2048,512]{0,1:T(8,128)} %maximum_select_fusion.1), channel_id=1, source_target_pairs={{0,2},{1,3},{2,0},{3,1},{4,6},{5,7},{6,4},{7,5},{8,10},{9,11},{10,... | collective-permute-start | bytes 12582920 | tf_op jit(solution)/shard_map/ppermute | solution.py:115
  1025.7 3.2 copy-start
Sparse Core Ops, SparseCore 0:
  407.5 96.1 all-gather.2
  1030.0 24.3 all-gather.4
